TPU v7x, 256 devices: a whole 4x4x8 slice. The times are simulated.
256 devices in a mesh: section: 4 (over z_hi, core), kv: 16 (over z_lo, y), tp: 4 (over x).
Axes of the slice: x: 4, y: 4, z: 8 (z_hi: 2, z_lo: 4; z = z_hi * 4 + z_lo), core: 2. Of those that a mesh axis runs over, the one named last changes fastest.
Arguments:
- patches: bfloat16 [32768, 1152], P(('section', 'kv'), 'tp'), may hold values from -6 to 6
- vis_gain: float32 [1152], replicated, may hold values from 0.1 to 1.9
- vis_bias: float32 [1152], replicated, may hold values from -3 to 3
- w_proj: bfloat16 [1152, 4608], P('section', 'tp')
- b_proj: float32 [4608], P('tp'), may hold values from -12 to 12
- rms_gain: float32 [4608], P('tp'), may hold values from 0.1 to 1.9
- w_kv: bfloat16 [4608, 2, 1024], P('tp'), may hold values from -0.09375 to 0.09375
- queries: bfloat16 [16, 2048], P('section', 'tp'), may hold values from -18 to 18
- cache: bfloat16 [1024, 128, 2, 1024], P(('section', 'kv'), None, None, 'tp'), may hold values from -6 to 6
- cache_lengths: int32 [4, 4], P('section'), may hold values from 1 to 31872, 32256 in all within a row
- slot_page: int32 [4, 256], P('section', 'kv'), may hold values from 0 to 255, each once within a row
- page_owner: int32 [4, 64], replicated, may hold values from 0 to 15, as said below
- image_request: int32 [4, 2], P('section'), may hold values from 0 to 3
Outputs:
- new_pages: bfloat16 [2048, 128, 2, 1024], P(('section', 'kv'), None, None, 'tp')
- attended: bfloat16 [16, 2048], P('section', 'tp')
Inputs may be any that keep to these rules, and one draw needn't show every extreme that they name: `page_owner`: from each source's 4 pages at most 2 go to any one owner; in every group one owner receives exactly 2 pages from every source.
All inputs are finite; a program needn't handle non-finite values.
Results may differ from a plain program's by a relative error of at most 0.0063.
Values may be sent and summed in bfloat16 or wider, within the bound.
No kernel may reach another device: no remote copies, remote signals or barrier semaphores. Data moves between devices by JAX's collectives and lax.ppermute only.
A program may use at most 64 MiB of HBM per device.

v0:
```python
import jax
import jax.numpy as jnp
from jax import lax
from jax.sharding import PartitionSpec as P

HEAD_DIM = 128
IMAGE_PAGES = 32
query_scale = 1.0 / 12.0
softcap = 50.0
epsilon = 1e-06


def laid_out(parts, dim):
    parts = jnp.moveaxis(parts, 0, dim)
    lengths = parts.shape
    return parts.reshape(*lengths[:dim], lengths[dim] * lengths[dim + 1], *lengths[dim + 2 :])


def sent_to_all(x, axis):
    copies = jnp.broadcast_to(x, (lax.axis_size(axis), *x.shape))
    return lax.all_to_all(copies, axis, split_axis=0, concat_axis=0, tiled=True)


def gather_directly(x, axis, dim):
    return laid_out(sent_to_all(x, axis), dim)


def over_copies(x, axis):
    everything = sent_to_all(x, axis)
    return jnp.sum(everything, axis=0)


def cut_along(x, dim, devices):
    before, after = (x.shape[:dim], x.shape[dim + 1 :])
    return jnp.moveaxis(x.reshape(*before, devices, -1, *after), dim, 0)


def summed_on_arrival(x, axis, dim):
    devices = lax.axis_size(axis)
    parts = lax.all_to_all(cut_along(x, dim, devices), axis, 0, 0, tiled=True)
    return jnp.sum(parts, axis=0)


def from_behind(value, axis, steps):
    count = lax.axis_size(axis)
    pairs = [(source, (source + steps) % count) for source in range(count)]
    return lax.ppermute(value, axis, pairs)


def together(arrays, axis):
    ends = [0]
    for a in arrays:
        ends.append(ends[-1] + a.size)
    subtotal = over_copies(jnp.concatenate([a.ravel() for a in arrays]), axis)
    return tuple((subtotal[b:e].reshape(a.shape) for a, b, e in zip(arrays, ends, ends[1:])))


def block_ranks(owners):
    per_block = owners.shape[1]
    same_owner = owners[:, :, None] == owners[:, None, :]
    earlier = jnp.arange(per_block)[None, :] < jnp.arange(per_block)[:, None]
    return jnp.sum((same_owner & earlier[None, :, :]).astype(jnp.int32), axis=2)


def attend_part(query_grid, page_store, token_mask):
    slot_count = page_store.shape[0]
    page_len = page_store.shape[1]
    head_count = page_store.shape[3] // HEAD_DIM
    keys = page_store[:, :, 0, :].reshape(slot_count * page_len, head_count, HEAD_DIM)
    values = page_store[:, :, 1, :].reshape(slot_count * page_len, head_count, HEAD_DIM)
    raw_scores = jnp.einsum("rkgd,tkd->rkgt", query_grid, keys, preferred_element_type=jnp.float32)
    capped = softcap * jnp.tanh(raw_scores * query_scale / softcap)
    allowed = token_mask.reshape(slot_count * page_len, -1).T
    weights = jnp.where(allowed[:, None, None, :], jnp.exp(capped), jnp.float32(0.0))
    totals = jnp.sum(weights, axis=3)
    weighted = jnp.einsum(
        "rkgt,tkd->rkgd", weights.astype(jnp.bfloat16), values, preferred_element_type=jnp.float32
    )
    return (totals, weighted)


def per_device(
    patches,
    vis_gain,
    vis_bias,
    w_proj,
    b_proj,
    rms_gain,
    w_kv,
    queries,
    cache,
    cache_lengths,
    slot_page,
    page_owner,
    image_request,
):
    kv_count = lax.axis_size("kv")
    section_idx = lax.axis_index("section")
    kv_idx = lax.axis_index("kv")
    row_count = patches.shape[0]
    page_len = cache.shape[1]
    pages_dev = row_count // page_len
    capacity = max(2, (2 * pages_dev + kv_count - 1) // kv_count)
    recv_slots = kv_count * capacity
    gathered = gather_directly(patches, "tp", 1).astype(jnp.float32)
    row_mean = jnp.mean(gathered, axis=1, keepdims=True)
    centred = gathered - row_mean
    variance = jnp.mean(centred * centred, axis=1, keepdims=True)
    x_norm = (centred * lax.rsqrt(variance + epsilon) * vis_gain + vis_bias).astype(jnp.bfloat16)
    projected = (
        jnp.dot(
            x_norm,
            lax.all_gather(w_proj, "section", axis=0, tiled=True),
            preferred_element_type=jnp.float32,
        )
        + b_proj
    )
    squares = over_copies(jnp.sum(projected * projected, axis=1), "tp")
    full_width = projected.shape[1] * lax.axis_size("tp")
    hidden = (projected * lax.rsqrt(squares / full_width + epsilon)[:, None] * rms_gain).astype(
        jnp.bfloat16
    )
    partial_kv = jnp.einsum("nd,dcf->ncf", hidden, w_kv, preferred_element_type=jnp.float32)
    image_kv = summed_on_arrival(partial_kv, "tp", 2)
    kv_pages = image_kv.astype(jnp.bfloat16).reshape(pages_dev, page_len, 2, image_kv.shape[2])
    handed = from_behind(kv_pages, "section", 1)
    owners = lax.dynamic_index_in_dim(page_owner, section_idx, 0, keepdims=False).reshape(
        kv_count, pages_dev
    )
    page_ranks = block_ranks(owners)
    my_owner = lax.dynamic_index_in_dim(owners, kv_idx, 0, keepdims=False)
    my_rank = lax.dynamic_index_in_dim(page_ranks, kv_idx, 0, keepdims=False)
    target = my_owner * capacity + my_rank
    placing = (jnp.arange(recv_slots)[:, None] == target[None, :]).astype(jnp.bfloat16)
    new_pages = lax.all_to_all(
        jnp.einsum("jp,ptcf->jtcf", placing, handed, preferred_element_type=jnp.float32).astype(
            jnp.bfloat16
        ),
        "kv",
        split_axis=0,
        concat_axis=0,
        tiled=True,
    )
    req_count = queries.shape[0]
    kv_heads_dev = cache.shape[3] // HEAD_DIM
    group_size = queries.shape[1] // HEAD_DIM // kv_heads_dev
    query_grid = queries.reshape(req_count, kv_heads_dev, group_size, HEAD_DIM)
    lengths = cache_lengths[0]
    page_counts = (lengths + page_len - 1) // page_len
    starts = jnp.cumsum(page_counts) - page_counts
    slot_ids = slot_page[0]
    within = slot_ids[:, None] - starts[None, :]
    inside = (within >= 0) & (within < page_counts[None, :])
    valid = jnp.where(inside, jnp.clip(lengths[None, :] - within * page_len, 0, page_len), 0)
    cache_mask = jnp.arange(page_len)[None, :, None] < valid[:, None, :]
    cache_totals, cache_weighted = attend_part(query_grid, cache, cache_mask)
    own_owners = lax.dynamic_index_in_dim(page_owner, section_idx, 0, keepdims=False).reshape(
        kv_count, pages_dev
    )
    own_ranks = block_ranks(own_owners)
    slot_of = (jnp.arange(kv_count)[:, None] * capacity + own_ranks).reshape(-1)
    arrives_here = own_owners.reshape(-1) == kv_idx
    image_count = image_request.shape[1]
    image_of = jnp.arange(kv_count * pages_dev) // IMAGE_PAGES
    request_row = image_request[0]
    page_request = jnp.sum(
        jnp.where(image_of[:, None] == jnp.arange(image_count)[None, :], request_row[None, :], 0),
        axis=1,
    )
    matched = arrives_here[None, :] & (slot_of[None, :] == jnp.arange(recv_slots)[:, None])
    request_hit = page_request[:, None] == jnp.arange(req_count)[None, :]
    slot_request = jnp.any(matched[:, :, None] & request_hit[None, :, :], axis=1)
    image_mask = jnp.broadcast_to(slot_request[:, None, :], (recv_slots, page_len, req_count))
    image_totals, image_weighted = attend_part(query_grid, new_pages, image_mask)
    totals, weighted = together(
        (cache_totals + image_totals, cache_weighted + image_weighted), "kv"
    )
    attended = (weighted / totals[..., None]).astype(jnp.bfloat16).reshape(req_count, -1)
    return (new_pages, attended)


def solution(mesh):
    in_specs = (
        P(("section", "kv"), "tp"),
        P(),
        P(),
        P("section", "tp"),
        P("tp"),
        P("tp"),
        P("tp", None, None),
        P("section", "tp"),
        P(("section", "kv"), None, None, "tp"),
        P("section", None),
        P("section", "kv"),
        P(),
        P("section", None),
    )
    out_specs = (P(("section", "kv"), None, None, "tp"), P("section", "tp"))
    return jax.shard_map(
        per_device, mesh=mesh, in_specs=in_specs, out_specs=out_specs, check_vma=False
    )
```

profile of v0, /device:TPU:2, one launch (start us, length us, event | category | flops | bytes accessed | tf_op | source)
XLA Modules:
  0.0 313.6 jit_solution(7396003237262253135)
XLA Ops:
  7.2 0.7 all-gather.2.cloned.1.call-update
  7.9 1.0 broadcast_in_dim.44
  9.0 19.7 %all_to_all.27 = bf16[4,512,288]{1,2,0:T(8,128)(2,1)S(1)} all-to-all(bf16[4,512,288]{1,2,0:T(8,128)(2,1)S(1)} %broadcast_in_dim.44), channel_id=1, replica_groups=mesh['section'=4,'kv'=16,'tp'=4] {'tp'}, dimensions={0} | all-to-all | bytes 2359296 | tf_op jit(solution)/shard_map/all_to_all | solution.py:21
  29.8 32.4 %all-gather.2.cloned.1.call-done = bf16[1152,1152]{1,0:T(8,128)(2,1)} async-done(((bf16[288,1152]{1,0:T(8,128)(2,1)}), bf16[1152,1152]{1,0:T(8,128)(2,1)}) %all-gather.2.cloned.1.call-update) | async-done | bytes 2654224 | tf_op jit(solution)/shard_map/all_gather | solution.py:113
  62.2 3.8 %multiply_reduce_fusion = (f32[512]{0:T(512)S(1)}, f32[512,1152]{1,0:T(8,128)S(1)}) fusion(f32[1152]{0:T(1024)S(1)} %copy-done.2, bf16[512,1152]{0,1:T(8,128)(2,1)S(1)} %fusion.10, bf16[1152,1152]{1,0:T(8,128)(2,1)} %all-gather.2.cloned.1.call-done), kind=kOutput, calls=%fused_computation.19 | convolution fusion | flops 1360723456 | bytes 6199808 | tf_op jit(solution)/shard_map/dot_general | solution.py:111
  66.0 8.5 %all_to_all.28 = f32[4,1,512]{2,1,0:T(1,128)S(1)} all-to-all(f32[4,1,512]{2,1,0:T(1,128)S(1)} %broadcast_in_dim.45), channel_id=1, replica_groups=mesh['section'=4,'kv'=16,'tp'=4] {'tp'}, dimensions={0} | all-to-all | bytes 16384 | tf_op jit(solution)/shard_map/all_to_all | solution.py:21
  74.5 5.3 %fusion = f32[512,2,1024]{2,0,1:T(8,128)S(1)} fusion(bf16[1152,2,1024]{2,1,0:T(2,128)(2,1)} %param.19, f32[512,1152]{1,0:T(8,128)S(1)} %get-tuple-element.11, f32[1152]{0:T(1024)} %param.18, f32[512]{0:T(512)S(1)} %add_rsqrt_fusion), kind=kOutput, calls=%fused_computation | convolution fusion | flops 2417688576 | bytes 11278848 | tf_op jit(solution)/shard_map/nd,dcf->ncf/dot_general | solution.py:123
  80.2 51.5 %all_to_all.29 = f32[4,512,2,256]{3,1,2,0:T(8,128)} all-to-all(f32[4,512,2,256]{3,1,2,0:T(8,128)S(1)} %bitcast.89), channel_id=1, replica_groups=mesh['section'=4,'kv'=16,'tp'=4] {'tp'}, dimensions={0} | all-to-all | bytes 8388608 | tf_op jit(solution)/shard_map/all_to_all | solution.py:40
  131.7 2.5 reduce_sum.99
  135.4 17.6 %collective-permute-done = bf16[4,128,2,256]{3,0,2,1:T(4,128)(2,1)S(1)} collective-permute-done((bf16[4,128,2,256]{3,0,2,1:T(4,128)(2,1)S(1)}, bf16[4,128,2,256]{3,0,2,1:T(4,128)(2,1)S(1)}, u32[]{:S(2)}, u32[]{:S(2)}) %collective-permute-start) | collective-permute-done | bytes 524320 | tf_op jit(solution)/shard_map/ppermute | solution.py:47
  153.0 1.4 convolution_convert_fusion
  154.3 6.3 %copy.97 = bf16[32,128,2,256]{3,2,1,0:T(2,128)(2,1)} copy(bf16[32,128,2,256]{3,0,2,1:T(8,128)(2,1)S(1)} %convolution_convert_fusion) | data formatting | bytes 8388608 | tf_op jit(solution)/shard_map/convert_element_type | solution.py:136
  160.7 4.9 %all-to-all-start.3 = ((bf16[32,128,2,256]{3,2,1,0:T(2,128)(2,1)}), bf16[32,128,2,256]{3,2,1,0:T(2,128)(2,1)}, u32[]{:S(2)}, u32[]{:S(2)}) async-start(bf16[32,128,2,256]{3,2,1,0:T(2,128)(2,1)} %copy.97), calls=%async_computation.3 | async-start | bytes 8388608 | tf_op jit(solution)/shard_map/all_to_all | solution.py:135
  166.2 10.0 %slice_reduce_fusion.3 = (bf16[16,128,256]{2,1,0:T(8,128)(2,1)}, bf16[16,128,256]{2,1,0:T(8,128)(2,1)S(1)}) fusion(bf16[16,128,2,256]{3,2,1,0:T(2,128)(2,1)S(1)} %copy-done.1), kind=kLoop, calls=%fused_computation.31 | loop fusion | bytes 4194304 | tf_op jit(solution)/shard_map/slice | solution.py:69
  176.2 1.4 reshape.276
  178.3 0.5 fusion.44
  179.0 60.3 %all-to-all-done.3 = bf16[32,128,2,256]{3,2,1,0:T(2,128)(2,1)} async-done(((bf16[32,128,2,256]{3,2,1,0:T(2,128)(2,1)}), bf16[32,128,2,256]{3,2,1,0:T(2,128)(2,1)}, u32[]{:S(2)}, u32[]{:S(2)}) %all-to-all-start.3) | async-done | bytes 4194336 | tf_op jit(solution)/shard_map/all_to_all | solution.py:135
  239.3 21.9 %slice_reduce_fusion.1 = (bf16[32,128,256]{2,1,0:T(8,128)(2,1)S(1)}, bf16[32,128,256]{2,1,0:T(8,128)(2,1)}) fusion(bf16[32,128,2,256]{3,2,1,0:T(2,128)(2,1)} %all-to-all-done.3), kind=kLoop, calls=%fused_computation.10 | loop fusion | bytes 8388608 | tf_op jit(solution)/shard_map/slice | solution.py:69
  261.2 2.1 reshape.277
  263.3 2.5 reshape.279
  265.8 2.3 fusion.45
  269.0 27.6 %all_to_all.30 = f32[16,1,2064]{2,1,0:T(1,128)S(1)} all-to-all(f32[16,1,2064]{2,1,0:T(1,128)S(1)} %broadcast_in_dim.54), channel_id=1, replica_groups=mesh['section'=4,'kv'=16,'tp'=4] {'kv'}, dimensions={0} | all-to-all | bytes 264192 | tf_op jit(solution)/shard_map/all_to_all | solution.py:21
  296.9 0.6 divide_convert_fusion
  297.5 9.2 %copy.166 = bf16[32,128,2,256]{3,2,1,0:T(2,128)(2,1)} copy(bf16[32,128,2,256]{3,2,1,0:T(2,128)(2,1)} %all-to-all-done.3) | data formatting | bytes 8388608
  (72 shorter events, 5.3 us)
Async XLA Ops:
  7.2 171.1 %copy-start = (bf16[4,512]{1,0:T(4,128)(2,1)S(1)}, bf16[4,512]{1,0:T(4,128)(2,1)}, u32[]{:S(2)}) copy-start(bf16[4,512]{1,0:T(4,128)(2,1)} %param.20) | copy-start | bytes 12292
  7.2 55.0 %all-gather.2.cloned.1.call-start = ((), (), s32[]{:S(2)}) async-start(), calls=%async_computation.5 | async-start | bytes 3317760 | tf_op jit(solution)/shard_map/all_gather | solution.py:113
  9.0 20.3 %copy-start.3 = (f32[1152]{0:T(1024)S(1)}, f32[1152]{0:T(1024)}, u32[]{:S(2)}) copy-start(f32[1152]{0:T(1024)} %param.15) | copy-start | bytes 13828
  9.0 20.3 %copy-start.4 = (f32[1152]{0:T(1024)S(1)}, f32[1152]{0:T(1024)}, u32[]{:S(2)}) copy-start(f32[1152]{0:T(1024)} %param.14) | copy-start | bytes 13828
  28.7 33.5 %copy-start.2 = (f32[1152]{0:T(1024)S(1)}, f32[1152]{0:T(1024)}, u32[]{:S(2)}) copy-start(f32[1152]{0:T(1024)} %param.17) | copy-start | bytes 13828
  131.6 3.2 %copy-start.7 = (s32[4,64]{1,0:T(4,128)S(1)}, s32[4,64]{1,0:T(4,128)}, u32[]{:S(2)}) copy-start(s32[4,64]{1,0:T(4,128)} %param.24) | copy-start | bytes 3076
  134.6 18.4 %collective-permute-start = (bf16[4,128,2,256]{3,0,2,1:T(4,128)(2,1)S(1)}, bf16[4,128,2,256]{3,0,2,1:T(4,128)(2,1)S(1)}, u32[]{:S(2)}, u32[]{:S(2)}) collective-permute-start(bf16[4,128,2,256]{3,0,2,1:T(4,128)(2,1)S(1)} %copy.96), channel_id=1, source_target_pairs={{0,64},{64,128},{128,192},{192,0},{1,65},{65,129},{129,193},{193,1... | collective-permute-start | bytes 1572872 | tf_op jit(solution)/shard_map/ppermute | solution.py:47
  160.7 5.1 %copy-start.8 = (s32[1,2]{1,0:T(1,128)S(1)}, s32[1,2]{1,0:T(1,128)}, u32[]{:S(2)}) copy-start(s32[1,2]{1,0:T(1,128)} %param.25) | copy-start | bytes 28
  160.7 5.5 %copy-start.1 = (bf16[16,128,2,256]{3,2,1,0:T(2,128)(2,1)S(1)}, bf16[16,128,2,256]{3,2,1,0:T(2,128)(2,1)}, u32[]{:S(2)}) copy-start(bf16[16,128,2,256]{3,2,1,0:T(2,128)(2,1)} %param.21) | copy-start | bytes 6291460
  160.7 78.6 %all-to-all-start.3 = ((bf16[32,128,2,256]{3,2,1,0:T(2,128)(2,1)}), bf16[32,128,2,256]{3,2,1,0:T(2,128)(2,1)}, u32[]{:S(2)}, u32[]{:S(2)}) async-start(bf16[32,128,2,256]{3,2,1,0:T(2,128)(2,1)} %copy.97), calls=%async_computation.3 | async-start | bytes 8388608 | tf_op jit(solution)/shard_map/all_to_all | solution.py:135
  166.2 11.3 %copy-start.5 = (s32[1,4]{1,0:T(1,128)S(1)}, s32[1,4]{1,0:T(1,128)}, u32[]{:S(2)}) copy-start(s32[1,4]{1,0:T(1,128)} %param.22) | copy-start | bytes 52
  176.2 1.9 copy-start.6
Sparse Core Ops, SparseCore 0:
  9.8 52.3 all-gather.1
where the time goes:
time: 314 us
  waiting for transfers between devices  111 us (35%)
  blocking collectives  107 us (34%)
  local copies, waits for them, and re-layouts  56.6 us (18%)
  between operations  14.4 us (5%)
  matrix products  14 us (4%)
  other arithmetic  5.3 us (2%)
  starting transfers between devices  5.19 us (2%)
    all_to_all x1, waiting for transfers between devices, per_device(): lax.all_to_all(jnp.einsum('jp,ptcf->jtcf', placing, handed, preferred_ele...  60.3 us
    all_to_all x3, blocking collectives, sent_to_all(): return lax.all_to_all(copies, axis, split_axis=0, concat_axis=0, tiled=True)  55.7 us
    all_to_all x1, blocking collectives, summed_on_arrival(): parts = lax.all_to_all(cut_along(x, dim, devices), axis, 0, 0, tiled=True)  51.5 us
    all_gather x1, waiting for transfers between devices, per_device(): lax.all_gather(w_proj, 'section', axis=0, tiled=True)  32.4 us
    slice x2, local copies, waits for them, and re-layouts, attend_part(): page_store[:, :, 0, :].reshape(slot_count * page_len, head_count, HEAD_DIM)  31.9 us
    ppermute x1, waiting for transfers between devices, from_behind(): return lax.ppermute(value, axis, pairs)  17.6 us
    unnamed x22, local copies, waits for them, and re-layouts  9.42 us
    convert_element_type x1, local copies, waits for them, and re-layouts, per_device(): jnp.einsum('jp,ptcf->jtcf', placing, handed, preferred_element_type=jnp.f...  6.33 us
  transfers between devices with their start and end apart: 3, of which 3 were waited for; matrix products, arithmetic and copies ran while one was open for 5% of the time, Pallas kernels for 0%

commit v1 on v0

--- a/solution.py
+++ b/solution.py
@@ -110,7 +110,10 @@
     projected = (
         jnp.dot(
             x_norm,
-            lax.all_gather(w_proj, "section", axis=0, tiled=True),
+            jnp.concatenate(
+                lax.all_to_all(jnp.stack([w_proj] * lax.axis_size("section")), "section", 0, 0),
+                axis=0,
+            ),
             preferred_element_type=jnp.float32,
         )
         + b_proj

time: 314 us -> 338 us (1.076)
  starting transfers between devices: 5.19 us -> 32.9 us
  waiting for transfers between devices: 111 us -> 136 us
  blocking collectives: 107 us -> 87.8 us
  between operations: 14.4 us -> 0.96 us
    all_to_all x0 -> x1, waiting for transfers between devices: none -> 62.6 us  [per_device(): lax.all_to_all(jnp.stack([w_proj] * lax.axis_size('section')), 'section',...]
    all_gather x1 -> x0, waiting for transfers between devices: 32.4 us -> none  [per_device(): lax.all_gather(w_proj, 'section', axis=0, tiled=True)]
    all_to_all x1, starting transfers between devices: 4.89 us -> 24 us  [per_device(): lax.all_to_all(jnp.einsum('jp,ptcf->jtcf', placing, handed, preferred_ele...]
    all_to_all x1, blocking collectives: 51.5 us -> 33 us  [summed_on_arrival(): parts = lax.all_to_all(cut_along(x, dim, devices), axis, 0, 0, tiled=True)]
    all_to_all x0 -> x1, starting transfers between devices: none -> 8.59 us  [per_device(): lax.all_to_all(jnp.stack([w_proj] * lax.axis_size('section')), 'section',...]
    ppermute x1, waiting for transfers between devices: 17.6 us -> 12 us  [from_behind(): return lax.ppermute(value, axis, pairs)]
    unnamed x22 -> x26, local copies, waits for them, and re-layouts: 9.42 us -> 9.42 us
  transfers between devices with their start and end apart: 3 -> 3, of which waited for: 3 -> 3; matrix products, arithmetic and copies ran while one was open for 5% -> 4% of each run, Pallas kernels for 0% -> 0%
where the time goes in v1:
time: 338 us; the launch traced here: 337 us
  waiting for transfers between devices  136 us (40%)
  blocking collectives  87.8 us (26%)
  local copies, waits for them, and re-layouts  58.5 us (17%)
  starting transfers between devices  32.9 us (10%)
  matrix products  16.2 us (5%)
  other arithmetic  4.85 us (1%)
    all_to_all x1, waiting for transfers between devices, per_device(): lax.all_to_all(jnp.stack([w_proj] * lax.axis_size('section')), 'section',...  62.6 us
    all_to_all x1, waiting for transfers between devices, per_device(): lax.all_to_all(jnp.einsum('jp,ptcf->jtcf', placing, handed, preferred_ele...  61.4 us
    all_to_all x3, blocking collectives, sent_to_all(): return lax.all_to_all(copies, axis, split_axis=0, concat_axis=0, tiled=True)  54.7 us
    all_to_all x1, blocking collectives, summed_on_arrival(): parts = lax.all_to_all(cut_along(x, dim, devices), axis, 0, 0, tiled=True)  33 us
    slice x2, local copies, waits for them, and re-layouts, attend_part(): page_store[:, :, 0, :].reshape(slot_count * page_len, head_count, HEAD_DIM)  31.9 us
    all_to_all x1, starting transfers between devices, per_device(): lax.all_to_all(jnp.einsum('jp,ptcf->jtcf', placing, handed, preferred_ele...  24 us
    ppermute x1, waiting for transfers between devices, from_behind(): return lax.ppermute(value, axis, pairs)  12 us
    unnamed x26, local copies, waits for them, and re-layouts  9.42 us
  transfers between devices with their start and end apart: 3, of which 3 were waited for; matrix products, arithmetic and copies ran while one was open for 4% of the time, Pallas kernels for 0%

profile of v1, /device:TPU:2, one launch (start us, length us, event | category | flops | bytes accessed | tf_op | source)
XLA Modules:
  0.0 337.1 jit_solution(8648048093821091158)
XLA Ops:
  0.7 1.1 broadcast_in_dim.44
  1.8 19.7 %all_to_all.32 = bf16[4,512,288]{1,2,0:T(8,128)(2,1)S(1)} all-to-all(bf16[4,512,288]{1,2,0:T(8,128)(2,1)S(1)} %broadcast_in_dim.44), channel_id=1, replica_groups=mesh['section'=4,'kv'=16,'tp'=4] {'tp'}, dimensions={0} | all-to-all | bytes 2359296 | tf_op jit(solution)/shard_map/all_to_all | solution.py:21
  21.4 1.7 stack.2
  23.1 8.6 %all-to-all-start.1 = ((bf16[4,288,1152]{2,1,0:T(8,128)(2,1)}), bf16[4,288,1152]{2,1,0:T(8,128)(2,1)}, u32[]{:S(2)}, u32[]{:S(2)}) async-start(bf16[4,288,1152]{2,1,0:T(8,128)(2,1)} %stack.2), calls=%async_computation.1 | async-start | bytes 5308416 | tf_op jit(solution)/shard_map/all_to_all | solution.py:114
  32.5 62.6 %all-to-all-done.1 = bf16[4,288,1152]{2,1,0:T(8,128)(2,1)} async-done(((bf16[4,288,1152]{2,1,0:T(8,128)(2,1)}), bf16[4,288,1152]{2,1,0:T(8,128)(2,1)}, u32[]{:S(2)}, u32[]{:S(2)}) %all-to-all-start.1) | async-done | bytes 2654240 | tf_op jit(solution)/shard_map/all_to_all | solution.py:114
  95.1 5.2 %multiply_reduce_fusion = (f32[512]{0:T(512)S(1)}, f32[512,1152]{1,0:T(8,128)}) fusion(f32[1152]{0:T(1024)S(1)} %copy-done.8, bf16[4,288,1152]{2,1,0:T(8,128)(2,1)} %all-to-all-done.1, bf16[4,512,288]{1,2,0:T(8,128)(2,1)S(1)} %all_to_all.32, f32[4,288]{1,0:T(4,128)S(1)} %add.109, f32[4,288]{1,0:T(4,128)S(1)} %mul.84, f32[512]{0:T(512)S(1)} %add_rsqrt_fusion.1, ...), kind=kOutput, calls=%fused_computation.23 | convolution fusion | flops 1364262400 | bytes 6213120 | tf_op jit(solution)/shard_map/dot_general | solution.py:111
  100.4 7.7 %all_to_all.33 = f32[4,1,512]{2,1,0:T(1,128)S(1)} all-to-all(f32[4,1,512]{2,1,0:T(1,128)S(1)} %broadcast_in_dim.45), channel_id=1, replica_groups=mesh['section'=4,'kv'=16,'tp'=4] {'tp'}, dimensions={0} | all-to-all | bytes 16384 | tf_op jit(solution)/shard_map/all_to_all | solution.py:21
  108.1 6.0 %fusion = f32[512,2,1024]{2,0,1:T(8,128)S(1)} fusion(bf16[1152,2,1024]{2,1,0:T(2,128)(2,1)} %param.19, f32[512,1152]{1,0:T(8,128)} %get-tuple-element.11, f32[1152]{0:T(1024)S(1)} %copy-done.9, f32[512]{0:T(512)S(1)} %add_rsqrt_fusion), kind=kOutput, calls=%fused_computation | convolution fusion | flops 2417688576 | bytes 11278848 | tf_op jit(solution)/shard_map/nd,dcf->ncf/dot_general | solution.py:126
  114.6 33.0 %all_to_all.34 = f32[4,512,2,256]{3,1,2,0:T(8,128)} all-to-all(f32[4,512,2,256]{3,1,2,0:T(8,128)S(1)} %bitcast.85), channel_id=1, replica_groups=mesh['section'=4,'kv'=16,'tp'=4] {'tp'}, dimensions={0} | all-to-all | bytes 8388608 | tf_op jit(solution)/shard_map/all_to_all | solution.py:40
  147.6 2.5 reduce_sum.99
  151.3 12.0 %collective-permute-done = bf16[4,128,2,256]{3,0,2,1:T(4,128)(2,1)S(1)} collective-permute-done((bf16[4,128,2,256]{3,0,2,1:T(4,128)(2,1)S(1)}, bf16[4,128,2,256]{3,0,2,1:T(4,128)(2,1)S(1)}, u32[]{:S(2)}, u32[]{:S(2)}) %collective-permute-start) | collective-permute-done | bytes 524320 | tf_op jit(solution)/shard_map/ppermute | solution.py:47
  163.3 1.4 convolution_convert_fusion
  164.7 6.3 %copy.96 = bf16[32,128,2,256]{3,2,1,0:T(2,128)(2,1)} copy(bf16[32,128,2,256]{3,0,2,1:T(8,128)(2,1)S(1)} %convolution_convert_fusion) | data formatting | bytes 8388608 | tf_op jit(solution)/shard_map/convert_element_type | solution.py:139
  171.0 24.0 %all-to-all-start.4 = ((bf16[32,128,2,256]{3,2,1,0:T(2,128)(2,1)}), bf16[32,128,2,256]{3,2,1,0:T(2,128)(2,1)}, u32[]{:S(2)}, u32[]{:S(2)}) async-start(bf16[32,128,2,256]{3,2,1,0:T(2,128)(2,1)} %copy.96), calls=%async_computation.4 | async-start | bytes 8388608 | tf_op jit(solution)/shard_map/all_to_all | solution.py:138
  195.7 10.0 %slice_reduce_fusion.3 = (bf16[16,128,256]{2,1,0:T(8,128)(2,1)}, bf16[16,128,256]{2,1,0:T(8,128)(2,1)S(1)}) fusion(bf16[16,128,2,256]{3,2,1,0:T(2,128)(2,1)S(1)} %copy-done.1), kind=kLoop, calls=%fused_computation.34 | loop fusion | bytes 4194304 | tf_op jit(solution)/shard_map/slice | solution.py:69
  205.7 1.4 reshape.298
  208.5 61.4 %all-to-all-done.4 = bf16[32,128,2,256]{3,2,1,0:T(2,128)(2,1)} async-done(((bf16[32,128,2,256]{3,2,1,0:T(2,128)(2,1)}), bf16[32,128,2,256]{3,2,1,0:T(2,128)(2,1)}, u32[]{:S(2)}, u32[]{:S(2)}) %all-to-all-start.4) | async-done | bytes 4194336 | tf_op jit(solution)/shard_map/all_to_all | solution.py:138
  269.9 21.9 %slice_reduce_fusion.1 = (bf16[32,128,256]{2,1,0:T(8,128)(2,1)S(1)}, bf16[32,128,256]{2,1,0:T(8,128)(2,1)}) fusion(bf16[32,128,2,256]{3,2,1,0:T(2,128)(2,1)} %all-to-all-done.4), kind=kLoop, calls=%fused_computation.10 | loop fusion | bytes 8388608 | tf_op jit(solution)/shard_map/slice | solution.py:69
  291.8 2.1 reshape.299
  293.9 2.5 reshape.301
  296.4 2.3 fusion.54
  299.6 27.4 %all_to_all.35 = f32[16,1,2064]{2,1,0:T(1,128)S(1)} all-to-all(f32[16,1,2064]{2,1,0:T(1,128)S(1)} %broadcast_in_dim.54), channel_id=1, replica_groups=mesh['section'=4,'kv'=16,'tp'=4] {'kv'}, dimensions={0} | all-to-all | bytes 264192 | tf_op jit(solution)/shard_map/all_to_all | solution.py:21
  327.3 0.6 divide_convert_fusion
  327.9 9.2 %copy.165 = bf16[32,128,2,256]{3,2,1,0:T(2,128)(2,1)} copy(bf16[32,128,2,256]{3,2,1,0:T(2,128)(2,1)} %all-to-all-done.4) | data formatting | bytes 8388608
  (77 shorter events, 5.5 us)
Async XLA Ops:
  0.6 207.1 %copy-start = (bf16[4,512]{1,0:T(4,128)(2,1)S(1)}, bf16[4,512]{1,0:T(4,128)(2,1)}, u32[]{:S(2)}) copy-start(bf16[4,512]{1,0:T(4,128)(2,1)} %param.20) | copy-start | bytes 12292
  0.6 20.8 %copy-start.2 = (bf16[288,1152]{1,0:T(8,128)(2,1)S(1)}, bf16[288,1152]{1,0:T(8,128)(2,1)}, u32[]{:S(2)}) copy-start(bf16[288,1152]{1,0:T(8,128)(2,1)} %param.16) | copy-start | bytes 1990660
  23.1 8.6 %copy-start.3 = (f32[1152]{0:T(1024)S(1)}, f32[1152]{0:T(1024)}, u32[]{:S(2)}) copy-start(f32[1152]{0:T(1024)} %param.15) | copy-start | bytes 13828
  23.1 8.7 %copy-start.4 = (f32[1152]{0:T(1024)S(1)}, f32[1152]{0:T(1024)}, u32[]{:S(2)}) copy-start(f32[1152]{0:T(1024)} %param.14) | copy-start | bytes 13828
  23.1 72.0 %all-to-all-start.1 = ((bf16[4,288,1152]{2,1,0:T(8,128)(2,1)}), bf16[4,288,1152]{2,1,0:T(8,128)(2,1)}, u32[]{:S(2)}, u32[]{:S(2)}) async-start(bf16[4,288,1152]{2,1,0:T(8,128)(2,1)} %stack.2), calls=%async_computation.1 | async-start | bytes 5308416 | tf_op jit(solution)/shard_map/all_to_all | solution.py:114
  31.7 63.4 %copy-start.8 = (f32[1152]{0:T(1024)S(1)}, f32[1152]{0:T(1024)}, u32[]{:S(2)}) copy-start(f32[1152]{0:T(1024)} %param.17) | copy-start | bytes 13828
  32.5 75.6 %copy-start.9 = (f32[1152]{0:T(1024)S(1)}, f32[1152]{0:T(1024)}, u32[]{:S(2)}) copy-start(f32[1152]{0:T(1024)} %param.18) | copy-start | bytes 13828
  147.6 3.2 copy-start.7
  150.5 12.8 %collective-permute-start = (bf16[4,128,2,256]{3,0,2,1:T(4,128)(2,1)S(1)}, bf16[4,128,2,256]{3,0,2,1:T(4,128)(2,1)S(1)}, u32[]{:S(2)}, u32[]{:S(2)}) collective-permute-start(bf16[4,128,2,256]{3,0,2,1:T(4,128)(2,1)S(1)} %copy.95), channel_id=1, source_target_pairs={{0,64},{64,128},{128,192},{192,0},{1,65},{65,129},{129,193},{193,1... | collective-permute-start | bytes 1572872 | tf_op jit(solution)/shard_map/ppermute | solution.py:47
  171.0 24.3 %copy-start.10 = (s32[1,2]{1,0:T(1,128)S(1)}, s32[1,2]{1,0:T(1,128)}, u32[]{:S(2)}) copy-start(s32[1,2]{1,0:T(1,128)} %param.25) | copy-start | bytes 28
  171.0 24.7 %copy-start.1 = (bf16[16,128,2,256]{3,2,1,0:T(2,128)(2,1)S(1)}, bf16[16,128,2,256]{3,2,1,0:T(2,128)(2,1)}, u32[]{:S(2)}) copy-start(bf16[16,128,2,256]{3,2,1,0:T(2,128)(2,1)} %param.21) | copy-start | bytes 6291460
  171.0 98.8 %all-to-all-start.4 = ((bf16[32,128,2,256]{3,2,1,0:T(2,128)(2,1)}), bf16[32,128,2,256]{3,2,1,0:T(2,128)(2,1)}, u32[]{:S(2)}, u32[]{:S(2)}) async-start(bf16[32,128,2,256]{3,2,1,0:T(2,128)(2,1)} %copy.96), calls=%async_computation.4 | async-start | bytes 8388608 | tf_op jit(solution)/shard_map/all_to_all | solution.py:138
  195.7 11.3 %copy-start.5 = (s32[1,4]{1,0:T(1,128)S(1)}, s32[1,4]{1,0:T(1,128)}, u32[]{:S(2)}) copy-start(s32[1,4]{1,0:T(1,128)} %param.22) | copy-start | bytes 52
  205.7 1.9 copy-start.6
